TPU v7x, 256 devices: a whole 4x4x8 slice. The times are simulated.
256 devices in a mesh: seq: 64 (over x, z, core), tp: 4 (over y).
Axes of the slice: x: 4, y: 4, z: 8, core: 2. Of those that a mesh axis runs over, the one named last changes fastest.
Arguments:
- hidden_in: bfloat16 [16384, 1536], P('seq', 'tp'), may hold values from -6 to 6
- w_in_gate: float32 [1536, 3072], P('seq', 'tp'), may hold values from -0.15625 to 0.15625
- w_in_value: float32 [1536, 3072], P('seq', 'tp'), may hold values from -0.15625 to 0.15625
- w_in_shared: float32 [1536, 256], P('seq'), may hold values from -0.15625 to 0.15625
- w_in_step: float32 [1536, 48], P('seq', 'tp'), may hold values from -0.15625 to 0.15625
- conv_value: float32 [4, 3072], P(None, 'tp'), may hold values from -3 to 3
- conv_shared: float32 [4, 256], replicated, may hold values from -3 to 3
- dt_bias: float32 [48], P('tp'), may hold values from -4 to -2
- a_log: float32 [48], P('tp'), may hold values from -8 to 0
- skip_gain: float32 [48], P('tp'), may hold values from 0.6 to 4.8
- norm_gain: float32 [3072], P('tp'), may hold values from 0.1 to 1.9
- w_out: float32 [3072, 1536], P('tp', 'seq'), may hold values from -0.109375 to 0.109375
- prompt_lengths: int32 [8], replicated, may hold values from 1 to 8192, 16384 in all
- row_blocks: int32 [64], replicated, may hold values from 0 to 63, each once
Outputs:
- mixed_out: bfloat16 [16384, 1536], P('seq', 'tp')
Inputs may be any that keep to these rules, and one draw needn't show every extreme that they name: `prompt_lengths`: 8 lengths that sum to 16384, the longest exactly 8192. `row_blocks`: a permutation of the row blocks.
All inputs are finite; a program needn't handle non-finite values.
Results may differ from a plain program's by a relative error of at most 0.02.
Values may be sent and summed in bfloat16 or wider, within the bound.
No kernel may reach another device: no remote copies, remote signals or barrier semaphores. Data moves between devices by JAX's collectives and lax.ppermute only.
A program may use at most 128 MiB of HBM per device.

v0:
```python
import jax
import jax.numpy as jnp
from jax import lax
from jax.sharding import PartitionSpec as P

EPSILON = 1e-05
HIGHEST_PREC = lax.Precision.HIGHEST


def passed_along(block, axis, distance):
    devices = range(lax.axis_size(axis))
    route = [(i - distance, i) for i in devices if i - distance in devices]
    return lax.ppermute(block, axis, route)


def prefix_2(x, axis, combine, identity):
    count, here = (lax.axis_size(axis), lax.axis_index(axis))
    everything = jax.tree.map(
        lambda part, kind: lax.all_gather(part.astype(kind), axis), x, (jnp.bfloat16, jnp.bfloat16)
    )
    start = jax.tree.map(
        lambda part, zero: jnp.broadcast_to(jnp.asarray(zero, part.dtype), part.shape), x, identity
    )

    def turn(k, before):
        reached = k < here
        new = combine(
            before, jax.tree.map(lambda part, own: part[k].astype(own.dtype), everything, x)
        )
        return jax.tree.map(lambda a, b: jnp.where(reached, a, b), new, before)

    return lax.fori_loop(0, count, turn, start)


def segment_of(positions, doc_ends):
    return jnp.sum((positions[:, None] >= doc_ends[None, :]).astype(jnp.int32), axis=1)


def span_parts(values, b_half, c_half, steps_dt, decay_rates, segments, prev_seg):
    length = values.shape[0]
    b_rows = b_half.astype(jnp.float32)
    cumulative = jnp.cumsum(-steps_dt * decay_rates[None, :], axis=0)
    places = jnp.arange(length)
    causal = (places[:, None] >= places[None, :]) & (segments[:, None] == segments[None, :])
    gaps_log = jnp.where(causal[:, :, None], cumulative[:, None, :] - cumulative[None, :, :], 0.0)
    decays_in = jnp.where(causal[:, :, None], jnp.exp(gaps_log), 0.0)
    scores = jnp.dot(c_half, b_half.T, preferred_element_type=jnp.float32)
    weights = scores[:, :, None] * decays_in * steps_dt[None, :, :]
    intra_part = jnp.einsum("ijh,jhp->ihp", weights, values, precision=HIGHEST_PREC)
    carry_in = jnp.where((segments == prev_seg)[:, None], jnp.exp(cumulative), 0.0)
    tail_weight = (
        jnp.where(
            (segments == segments[-1])[:, None], jnp.exp(cumulative[-1][None, :] - cumulative), 0.0
        )
        * steps_dt
    )
    fresh_state = jnp.einsum("jh,jhp,jn->hpn", tail_weight, values, b_rows, precision=HIGHEST_PREC)
    keep_factor = jnp.where(segments[-1] == prev_seg, jnp.exp(cumulative[-1]), 0.0)
    return (intra_part, carry_in, fresh_state, keep_factor)


def combine(earlier, later):
    return (earlier[0] * later[0], later[0][:, None, None] * earlier[1] + later[1])


def on_device(
    hidden_in,
    w_in_gate,
    w_in_value,
    w_in_shared,
    w_in_step,
    conv_value,
    conv_shared,
    dt_bias,
    a_log,
    skip_gain,
    norm_gain,
    w_out,
    prompt_lengths,
    row_blocks,
):
    seq_count = lax.axis_size("seq")
    tokens_here = hidden_in.shape[0]
    edge_count = conv_value.shape[0] - 1
    gathered = lax.all_gather(hidden_in, "tp", axis=1, tiled=True)
    row_count = gathered.shape[0]
    model_width = gathered.shape[1]
    permuted = jnp.take(
        gathered.reshape(row_count, seq_count, model_width // seq_count), row_blocks, axis=1
    ).reshape(row_count, model_width)
    stored = (
        w_in_gate.astype(jnp.bfloat16),
        w_in_value.astype(jnp.bfloat16),
        w_in_shared.astype(jnp.bfloat16),
        w_in_step.astype(jnp.bfloat16),
    )
    pieces = (
        lax.all_gather(stored[0], "seq", axis=0, tiled=True),
        lax.all_gather(stored[1], "seq", axis=0, tiled=True),
        lax.all_gather(stored[2], "seq", axis=0, tiled=True),
        lax.all_gather(stored[3], "seq", axis=0, tiled=True),
    )
    projected = tuple(
        (
            jnp.dot(permuted, weight_piece, preferred_element_type=jnp.float32)
            for weight_piece in pieces
        )
    )
    gate_all, value_all, shared_all, raw_all = [result.astype(jnp.bfloat16) for result in projected]
    mixed_in = jnp.concatenate([value_all, shared_all], axis=1)
    edge_mix = passed_along(mixed_in[tokens_here - edge_count :], "seq", 1)
    doc_ends = jnp.cumsum(prompt_lengths)
    first_pos = lax.axis_index("seq") * tokens_here
    positions = first_pos + jnp.arange(tokens_here, dtype=jnp.int32)
    edge_positions = first_pos - edge_count + jnp.arange(edge_count, dtype=jnp.int32)
    segments = segment_of(positions, doc_ends)
    ext_segments = jnp.concatenate([segment_of(edge_positions, doc_ends), segments])
    ext_rows = jnp.concatenate([edge_mix, mixed_in], axis=0)
    kernel = jnp.concatenate([conv_value, conv_shared], axis=1)
    conv_sum = jnp.zeros(mixed_in.shape, jnp.float32)
    for tap_index in range(edge_count + 1):
        same_doc = (ext_segments[tap_index : tap_index + tokens_here] == segments)[:, None]
        conv_sum = conv_sum + jnp.where(
            same_doc,
            kernel[tap_index][None, :]
            * ext_rows[tap_index : tap_index + tokens_here].astype(jnp.float32),
            0.0,
        )
    convolved = jax.nn.silu(conv_sum).astype(jnp.bfloat16)
    local_inner = conv_value.shape[1]
    local_heads = dt_bias.shape[0]
    head_dim = local_inner // local_heads
    state_size = conv_shared.shape[1] // 2
    values = (
        convolved[:, :local_inner].astype(jnp.float32).reshape(tokens_here, local_heads, head_dim)
    )
    b_half = convolved[:, local_inner : local_inner + state_size]
    c_half = convolved[:, local_inner + state_size :]
    c_rows = c_half.astype(jnp.float32)
    steps_dt = jax.nn.softplus(raw_all.astype(jnp.float32) + dt_bias[None, :])
    decay_rates = jnp.exp(a_log)
    prev_first = segment_of(jnp.reshape(first_pos - 1, (1,)), doc_ends)[0]
    device_keep = jnp.ones((local_heads,), jnp.float32)
    device_state = jnp.zeros((local_heads, head_dim, state_size), jnp.float32)
    parts = span_parts(values, b_half, c_half, steps_dt, decay_rates, segments, prev_first)
    device_keep = parts[3] * device_keep
    device_state = parts[3][:, None, None] * device_state + parts[2]
    identity = (jnp.ones_like(device_keep), jnp.zeros_like(device_state))
    prefix = prefix_2((device_keep, device_state), "seq", combine, identity)
    carried = prefix[1]
    intra_part, carry_in, fresh_state, keep_factor = parts
    inter_part = (
        jnp.einsum("in,hpn->ihp", c_rows, carried, precision=HIGHEST_PREC) * carry_in[:, :, None]
    )
    outputs = intra_part + inter_part
    mixed_heads = outputs + skip_gain[None, :, None] * values
    gated = mixed_heads.reshape(tokens_here, local_inner) * jax.nn.silu(
        gate_all.astype(jnp.float32)
    )
    squares = jnp.sum(gated * gated, axis=1)
    square_total = lax.psum(squares, "tp")
    mean_square = square_total / (local_inner * lax.axis_size("tp"))
    normed = (gated * lax.rsqrt(mean_square + EPSILON)[:, None] * norm_gain[None, :]).astype(
        jnp.bfloat16
    )
    out_weight = w_out.astype(jnp.bfloat16)
    partial_terms = jnp.dot(
        normed,
        lax.all_gather(out_weight, "seq", axis=1, tiled=True),
        preferred_element_type=jnp.float32,
    )
    return lax.psum_scatter(
        partial_terms.astype(jnp.bfloat16), "tp", scatter_dimension=1, tiled=True
    )


def solution(mesh):
    return jax.shard_map(
        on_device,
        mesh=mesh,
        in_specs=(
            P("seq", "tp"),
            P("seq", "tp"),
            P("seq", "tp"),
            P("seq", None),
            P("seq", "tp"),
            P(None, "tp"),
            P(),
            P("tp"),
            P("tp"),
            P("tp"),
            P("tp"),
            P("tp", "seq"),
            P(),
            P(),
        ),
        out_specs=P("seq", "tp"),
        check_vma=False,
    )
```

profile of v0, /device:TPU:2, one launch (start us, length us, event | category | flops | bytes accessed | tf_op | source)
XLA Modules:
  0.0 420.0 jit_solution(3729731392679539498)
XLA Ops:
  6.5 1.5 convert_element_type.112
  9.6 1.1 copy.39
  13.0 46.7 %all-gather.1 = bf16[64,24,12]{1,2,0:T(8,128)(2,1)S(1)} all-gather(bf16[1,24,12]{1,2,0:T(8,128)(2,1)S(1)} %convert_bitcast_fusion), channel_id=1, replica_groups=mesh['seq'=64,'tp'=4] {'seq'}, dimensions={0}, use_global_device_ids=true | all-gather | bytes 37440 | tf_op jit(solution)/shard_map/all_gather | solution.py:101
  61.4 14.2 %all_gather.28 = bf16[256,1536]{0,1:T(8,128)(2,1)S(1)} all-gather(bf16[256,384]{0,1:T(8,128)(2,1)S(1)} %copy.39), channel_id=1, replica_groups=mesh['seq'=64,'tp'=4] {'tp'}, dimensions={1}, use_global_device_ids=true | all-gather | bytes 983040 | tf_op jit(solution)/shard_map/all_gather | solution.py:85
  80.0 48.3 %all_gather.30 = bf16[1536,256]{1,0:T(8,128)(2,1)S(1)} all-gather(bf16[24,256]{1,0:T(8,128)(2,1)S(1)} %convert_element_type.114), channel_id=1, replica_groups=mesh['seq'=64,'tp'=4] {'seq'}, dimensions={0}, use_global_device_ids=true | all-gather | bytes 798720 | tf_op jit(solution)/shard_map/all_gather | solution.py:100
  128.3 1.3 broadcast_compare_fusion
  130.1 2.5 convolution_convert_fusion.2
  132.6 2.3 collective-permute-start
  134.9 4.8 %collective-permute-done = bf16[3,1024]{1,0:T(4,128)(2,1)S(1)} collective-permute-done((bf16[3,1024]{1,0:T(4,128)(2,1)S(1)}, bf16[3,1024]{1,0:T(4,128)(2,1)S(1)}, u32[]{:S(2)}, u32[]{:S(2)}) %collective-permute-start) | collective-permute-done | bytes 6176 | tf_op jit(solution)/shard_map/ppermute | solution.py:13
  140.9 1.2 fusion.20
  143.9 38.1 %all-gather.2 = bf16[64,1,12]{2,1,0:T(2,128)(2,1)S(1)} all-gather(bf16[1,1,12]{2,1,0:T(2,128)(2,1)S(1)} %bitcast.96), channel_id=1, replica_groups=mesh['seq'=64,'tp'=4] {'seq'}, dimensions={0}, use_global_device_ids=true | all-gather | bytes 1560 | tf_op jit(solution)/shard_map/all_gather | solution.py:19
  182.2 3.6 fusion.14
  185.8 43.4 %all-gather.14.cloned.1.call-done = bf16[768,64,128]{2,1,0:T(8,128)(2,1)} async-done(((bf16[12,64,128]{2,1,0:T(8,128)(2,1)}), bf16[768,64,128]{2,1,0:T(8,128)(2,1)}) %all-gather.14.cloned.1.call-update) | async-done | bytes 12582928 | tf_op jit(solution)/shard_map/all_gather | solution.py:19
  229.1 70.1 %while.14 = (s32[]{:T(128)}, f32[12,64,128]{2,1,0:T(8,128)S(1)}, s32[]{:T(128)}, bf16[64,12]{1,0:T(8,128)(2,1)S(1)}, bf16[64,12,64,128]{3,2,1,0:T(8,128)(2,1)}, /*index=5*/s32[]{:T(128)}, s32[]{:T(128)}) while((s32[]{:T(128)}, f32[12,64,128]{2,1,0:T(8,128)S(1)}, s32[]{:T(128)}, bf16[64,12]{1,0:T(8,128)(2,1)S(1)}, ...), condition=%wide.region_7.8_spmd.clone, body=%wide.region_6.7_spmd.clone.sunk | while | flops 491536 | bytes 983265 | solution.py:32
  229.2 1.1 fusion.58
  230.2 1.1 fusion.58
  231.3 1.1 fusion.58
  233.5 1.1 fusion.58
  234.6 1.1 fusion.58
  235.7 1.1 fusion.58
  236.8 1.1 fusion.58
  237.9 1.1 fusion.58
  239.0 1.1 fusion.58
  240.1 1.1 fusion.58
  241.2 1.1 fusion.58
  242.3 1.1 fusion.58
  244.5 1.1 fusion.58
  245.6 1.1 fusion.58
  246.7 1.1 fusion.58
  247.7 1.1 fusion.58
  248.8 1.1 fusion.58
  251.0 1.1 fusion.58
  265.3 1.1 fusion.58
  278.4 1.1 fusion.58
  283.9 1.1 fusion.58
  287.2 1.1 fusion.58
  294.9 1.1 fusion.58
  296.0 1.1 fusion.58
  298.2 1.1 fusion.58
  299.3 1.6 fusion.18
  301.2 5.5 %all-gather.10.cloned.1.call-done = bf16[1536,768]{1,0:T(8,128)(2,1)} async-done(((bf16[24,768]{1,0:T(8,128)(2,1)}), bf16[1536,768]{1,0:T(8,128)(2,1)}) %all-gather.10.cloned.1.call-update) | async-done | bytes 2359312 | tf_op jit(solution)/shard_map/all_gather | solution.py:98
  306.7 2.7 multiply_reduce_fusion
  309.4 10.5 %psum.7 = f32[256]{0:T(256)S(1)} all-reduce(f32[256]{0:T(256)S(1)} %get-tuple-element.160), channel_id=1, replica_groups=mesh['seq'=64,'tp'=4] {'tp'}, use_global_device_ids=true, to_apply=%region_9.10 | all-reduce | flops 256 | bytes 2048 | tf_op jit(solution)/shard_map/psum | solution.py:161
  319.8 64.6 %all-gather.12.cloned.1.call-done = bf16[768,1536]{0,1:T(8,128)(2,1)} async-done(((bf16[768,24]{0,1:T(8,128)(2,1)}), bf16[768,1536]{0,1:T(8,128)(2,1)}) %all-gather.12.cloned.1.call-update) | async-done | bytes 2359312 | tf_op jit(solution)/shard_map/all_gather | solution.py:169
  384.4 2.5 convolution_convert_fusion
  386.9 1.2 copy.50
  388.1 23.7 %reduce-scatter.4.cloned.1.call-done = bf16[384,256]{1,0:T(8,128)(2,1)} async-done(((bf16[1536,256]{1,0:T(8,128)(2,1)}), bf16[384,256]{1,0:T(8,128)(2,1)}) %reduce-scatter.4.cloned.1.call-update) | async-done | bytes 196624
  411.8 1.7 copy.51
  (180 shorter events, 54.2 us)
Async XLA Ops:
  6.5 123.6 %all-gather.8.cloned.1.call-start = ((), (), s32[]{:S(2)}) async-start(), calls=%async_computation.1 | async-start | bytes 2396160 | tf_op jit(solution)/shard_map/all_gather | solution.py:99
  8.1 221.1 %all-gather.14.cloned.1.call-start = ((), (), s32[]{:S(2)}) async-start(), calls=%async_computation.4 | async-start | bytes 12779520 | tf_op jit(solution)/shard_map/all_gather | solution.py:19
  75.6 0.9 copy-start.5
  76.2 3.6 copy-start.2
  76.2 3.6 copy-start.4
  132.6 7.1 %collective-permute-start = (bf16[3,1024]{1,0:T(4,128)(2,1)S(1)}, bf16[3,1024]{1,0:T(4,128)(2,1)S(1)}, u32[]{:S(2)}, u32[]{:S(2)}) collective-permute-start(bf16[3,1024]{1,0:T(4,128)(2,1)S(1)} %fusion.40), channel_id=1, source_target_pairs={{0,4},{4,8},{8,12},{12,16},{16,20},{20,24},{24,28},{28,32},{32,36}... | collective-permute-start | bytes 18440 | tf_op jit(solution)/shard_map/ppermute | solution.py:13
  139.9 2.3 copy-start
  139.9 3.1 copy-start.1
  142.2 164.5 %all-gather.10.cloned.1.call-start = ((), (), s32[]{:S(2)}) async-start(), calls=%async_computation.2 | async-start | bytes 2396160 | tf_op jit(solution)/shard_map/all_gather | solution.py:98
  142.9 241.5 %all-gather.12.cloned.1.call-start = ((), (), s32[]{:S(2)}) async-start(), calls=%async_computation.3 | async-start | bytes 2396160 | tf_op jit(solution)/shard_map/all_gather | solution.py:169
  143.6 268.2 %reduce-scatter.4.cloned.1.call-start = ((), (), s32[]{:S(2)}) async-start(), calls=%async_computation.5 | async-start | bytes 983040
  229.1 70.1 %copy-start.6 = (f32[12]{0:T(128)S(1)}, f32[12]{0:T(128)}, u32[]{:S(2)}) copy-start(f32[12]{0:T(128)} %param.25) | copy-start | bytes 148
  301.2 83.2 %copy-start.3 = (f32[768]{0:T(1024)S(1)}, f32[768]{0:T(1024)}, u32[]{:S(2)}) copy-start(f32[768]{0:T(1024)} %param.26) | copy-start | bytes 9220
Sparse Core Ops, SparseCore 0:
  10.1 79.4 all-gather.7
  142.3 86.8 all-gather.13
  231.8 74.7 all-gather.9
  309.2 75.1 all-gather.11
  388.2 23.5 reduce-scatter.3
where the time goes:
time: 422 us; the launch traced here: 420 us
  blocking collectives  158 us (37%)
  waiting for transfers between devices  142 us (34%)
  other arithmetic  79 us (19%)
  matrix products  14.9 us (4%)
  between operations  14.6 us (3%)
  local copies, waits for them, and re-layouts  7.21 us (2%)
    select_n x64, other arithmetic, turn(): return jax.tree.map(lambda a, b: jnp.where(reached, a, b), new, before)  67.4 us
    all_gather x1, waiting for transfers between devices, on_device(): lax.all_gather(out_weight, 'seq', axis=1, tiled=True)  64.6 us
    all_gather x1, blocking collectives, on_device(): lax.all_gather(stored[2], 'seq', axis=0, tiled=True)  48.3 us
    all_gather x1, blocking collectives, on_device(): lax.all_gather(stored[3], 'seq', axis=0, tiled=True)  46.7 us
    all_gather x1, waiting for transfers between devices, prefix_2(): lax.all_gather(part.astype(kind), axis)  43.4 us
    all_gather x1, blocking collectives, prefix_2(): lax.all_gather(part.astype(kind), axis)  38.1 us
    unnamed x6, waiting for transfers between devices  23.8 us
    all_gather x1, blocking collectives, on_device(): gathered = lax.all_gather(hidden_in, 'tp', axis=1, tiled=True)  14.2 us
  transfers between devices with their start and end apart: 6, of which 5 were waited for; matrix products, arithmetic and copies ran while one was open for 21% of the time, Pallas kernels for 0%

commit v1 on v0

--- a/solution.py
+++ b/solution.py
@@ -5,6 +5,11 @@
 
 EPSILON = 1e-05
 HIGHEST_PREC = lax.Precision.HIGHEST
+
+
+def tiled_gather(value, axis, dim):
+    copies = jnp.concatenate([value] * lax.axis_size(axis), axis=dim)
+    return lax.all_to_all(copies, axis, dim, dim, tiled=True)
 
 
 def passed_along(block, axis, distance):
@@ -165,9 +170,7 @@
     )
     out_weight = w_out.astype(jnp.bfloat16)
     partial_terms = jnp.dot(
-        normed,
-        lax.all_gather(out_weight, "seq", axis=1, tiled=True),
-        preferred_element_type=jnp.float32,
+        normed, tiled_gather(out_weight, "seq", 1), preferred_element_type=jnp.float32
     )
     return lax.psum_scatter(
         partial_terms.astype(jnp.bfloat16), "tp", scatter_dimension=1, tiled=True

time: 422 us -> 378 us (0.90)
  waiting for transfers between devices: 142 us -> 24.7 us
  blocking collectives: 158 us -> 218 us
  starting transfers between devices: 2.43 us -> 9.7 us
    all_gather x1 -> x0, waiting for transfers between devices: 64.6 us -> none  [on_device(): lax.all_gather(out_weight, 'seq', axis=1, tiled=True)]
    all_gather x1, blocking collectives: 38.1 us -> 97.5 us  [prefix_2(): lax.all_gather(part.astype(kind), axis)]
    all_gather x1, waiting for transfers between devices: 43.4 us -> 0.01 us  [prefix_2(): lax.all_gather(part.astype(kind), axis)]
    all_to_all x0 -> x1, starting transfers between devices: none -> 7.32 us  [tiled_gather(): return lax.all_to_all(copies, axis, dim, dim, tiled=True)]
    all_gather x1, waiting for transfers between devices: 5.49 us -> 0.02 us  [on_device(): lax.all_gather(stored[0], 'seq', axis=0, tiled=True)]
    unnamed x6 -> x5, waiting for transfers between devices: 23.8 us -> 19.8 us
  transfers between devices with their start and end apart: 6 -> 6, of which waited for: 5 -> 2; matrix products, arithmetic and copies ran while one was open for 21% -> 25% of each run, Pallas kernels for 0% -> 0%
where the time goes in v1:
time: 378 us; the launch traced here: 375 us
  blocking collectives  218 us (58%)
  other arithmetic  78.4 us (21%)
  waiting for transfers between devices  24.7 us (7%)
  matrix products  17.3 us (5%)
  between operations  15.2 us (4%)
  local copies, waits for them, and re-layouts  10.1 us (3%)
  starting transfers between devices  9.7 us (3%)
    all_gather x1, blocking collectives, prefix_2(): lax.all_gather(part.astype(kind), axis)  97.5 us
    select_n x64, other arithmetic, turn(): return jax.tree.map(lambda a, b: jnp.where(reached, a, b), new, before)  67.3 us
    all_gather x1, blocking collectives, on_device(): lax.all_gather(stored[2], 'seq', axis=0, tiled=True)  48.3 us
    all_gather x1, blocking collectives, on_device(): lax.all_gather(stored[3], 'seq', axis=0, tiled=True)  46.7 us
    unnamed x5, waiting for transfers between devices  19.8 us
    all_gather x1, blocking collectives, on_device(): gathered = lax.all_gather(hidden_in, 'tp', axis=1, tiled=True)  14.2 us
    psum x1, blocking collectives, on_device(): square_total = lax.psum(squares, 'tp')  11.4 us
  transfers between devices with their start and end apart: 6, of which 2 were waited for; matrix products, arithmetic and copies ran while one was open for 25% of the time, Pallas kernels for 0%

profile of v1, /device:TPU:2, one launch (start us, length us, event | category | flops | bytes accessed | tf_op | source)
XLA Modules:
  0.0 375.5 jit_solution(15339922323514911730)
XLA Ops:
  6.5 1.5 convert_element_type.112
  9.6 1.1 copy.39
  13.0 46.7 %all-gather.1 = bf16[64,24,12]{1,2,0:T(8,128)(2,1)S(1)} all-gather(bf16[1,24,12]{1,2,0:T(8,128)(2,1)S(1)} %convert_bitcast_fusion), channel_id=1, replica_groups=mesh['seq'=64,'tp'=4] {'seq'}, dimensions={0}, use_global_device_ids=true | all-gather | bytes 37440 | tf_op jit(solution)/shard_map/all_gather | solution.py:106
  61.4 14.2 %all_gather.25 = bf16[256,1536]{0,1:T(8,128)(2,1)S(1)} all-gather(bf16[256,384]{0,1:T(8,128)(2,1)S(1)} %copy.39), channel_id=1, replica_groups=mesh['seq'=64,'tp'=4] {'tp'}, dimensions={1}, use_global_device_ids=true | all-gather | bytes 983040 | tf_op jit(solution)/shard_map/all_gather | solution.py:90
  80.1 48.3 %all_gather.27 = bf16[1536,256]{1,0:T(8,128)(2,1)S(1)} all-gather(bf16[24,256]{1,0:T(8,128)(2,1)S(1)} %convert_element_type.114), channel_id=1, replica_groups=mesh['seq'=64,'tp'=4] {'seq'}, dimensions={0}, use_global_device_ids=true | all-gather | bytes 798720 | tf_op jit(solution)/shard_map/all_gather | solution.py:105
  128.5 1.3 broadcast_compare_fusion
  130.3 2.5 convolution_convert_fusion.2
  132.8 2.3 collective-permute-start
  135.1 4.8 %collective-permute-done = bf16[3,1024]{1,0:T(4,128)(2,1)S(1)} collective-permute-done((bf16[3,1024]{1,0:T(4,128)(2,1)S(1)}, bf16[3,1024]{1,0:T(4,128)(2,1)S(1)}, u32[]{:S(2)}, u32[]{:S(2)}) %collective-permute-start) | collective-permute-done | bytes 6176 | tf_op jit(solution)/shard_map/ppermute | solution.py:18
  141.1 1.2 fusion.20
  143.2 1.4 copy-done.2
  144.7 7.3 %all-to-all-start = ((bf16[768,64,24]{0,2,1:T(8,128)(2,1)}), bf16[768,64,24]{0,2,1:T(8,128)(2,1)S(1)}, u32[]{:S(2)}, u32[]{:S(2)}) async-start(bf16[768,64,24]{0,2,1:T(8,128)(2,1)} %bitcast.87), calls=%async_computation | async-start | bytes 4718592 | tf_op jit(solution)/shard_map/all_to_all | solution.py:12
  153.1 97.5 %all-gather.2 = bf16[64,1,12]{2,1,0:T(2,128)(2,1)S(1)} all-gather(bf16[1,1,12]{2,1,0:T(2,128)(2,1)S(1)} %bitcast.100), channel_id=1, replica_groups=mesh['seq'=64,'tp'=4] {'seq'}, dimensions={0}, use_global_device_ids=true | all-gather | bytes 1560 | tf_op jit(solution)/shard_map/all_gather | solution.py:24
  250.6 1.1 fusion.30
  251.6 3.6 fusion.14
  255.2 70.0 %while.14 = (s32[]{:T(128)}, f32[12,64,128]{2,1,0:T(8,128)S(1)}, s32[]{:T(128)}, bf16[64,12]{1,0:T(8,128)(2,1)S(1)}, bf16[64,12,64,128]{3,2,1,0:T(8,128)(2,1)}, /*index=5*/s32[]{:T(128)}, s32[]{:T(128)}) while((s32[]{:T(128)}, f32[12,64,128]{2,1,0:T(8,128)S(1)}, s32[]{:T(128)}, bf16[64,12]{1,0:T(8,128)(2,1)S(1)}, ...), condition=%wide.region_7.8_spmd.clone, body=%wide.region_6.7_spmd.clone.sunk | while | flops 491536 | bytes 983265 | solution.py:37
  255.2 1.1 fusion.58
  256.3 1.1 fusion.58
  257.4 1.1 fusion.58
  258.5 1.1 fusion.58
  259.6 1.1 fusion.58
  260.7 1.1 fusion.58
  261.8 1.1 fusion.58
  262.9 1.1 fusion.58
  264.0 1.1 fusion.58
  265.1 1.1 fusion.58
  266.2 1.1 fusion.58
  267.3 1.1 fusion.58
  268.3 1.1 fusion.58
  269.4 1.1 fusion.58
  270.5 1.1 fusion.58
  271.6 1.1 fusion.58
  272.7 1.1 fusion.58
  278.2 1.1 fusion.58
  281.5 1.1 fusion.58
  301.2 1.1 fusion.58
  307.7 1.1 fusion.58
  311.0 1.1 fusion.58
  316.5 1.1 fusion.58
  318.7 1.1 fusion.58
  325.2 2.6 fusion.18
  327.8 1.4 copy.47
  329.3 3.7 multiply_reduce_fusion
  333.0 11.4 %psum.7 = f32[256]{0:T(256)S(1)} all-reduce(f32[256]{0:T(256)S(1)} %get-tuple-element.162), channel_id=1, replica_groups=mesh['seq'=64,'tp'=4] {'tp'}, use_global_device_ids=true, to_apply=%region_9.10 | all-reduce | flops 256 | bytes 2048 | tf_op jit(solution)/shard_map/psum | solution.py:166
  344.4 2.0 convolution_convert_fusion
  346.3 1.2 copy.50
  347.5 19.7 %reduce-scatter.4.cloned.1.call-done = bf16[384,256]{1,0:T(8,128)(2,1)} async-done(((bf16[1536,256]{1,0:T(8,128)(2,1)}), bf16[384,256]{1,0:T(8,128)(2,1)}) %reduce-scatter.4.cloned.1.call-update) | async-done | bytes 196624
  367.2 1.7 copy.51
  (248 shorter events, 54.6 us)
Async XLA Ops:
  6.5 123.8 %all-gather.7.cloned.1.call-start = ((), (), s32[]{:S(2)}) async-start(), calls=%async_computation.2 | async-start | bytes 2396160 | tf_op jit(solution)/shard_map/all_gather | solution.py:104
  8.1 247.1 %all-gather.11.cloned.1.call-start = ((), (), s32[]{:S(2)}) async-start(), calls=%async_computation.4 | async-start | bytes 12779520 | tf_op jit(solution)/shard_map/all_gather | solution.py:24
  75.6 0.9 copy-start.8
  76.2 3.7 copy-start.5
  76.2 3.7 copy-start.7
  76.5 56.3 %copy-start = (bf16[256,1536]{0,1:T(8,128)(2,1)}, bf16[256,1536]{0,1:T(8,128)(2,1)S(1)}, u32[]{:S(2)}) copy-start(bf16[256,1536]{0,1:T(8,128)(2,1)S(1)} %bitcast_select_fusion) | copy-start | bytes 2359300
  132.8 7.1 %collective-permute-start = (bf16[3,1024]{1,0:T(4,128)(2,1)S(1)}, bf16[3,1024]{1,0:T(4,128)(2,1)S(1)}, u32[]{:S(2)}, u32[]{:S(2)}) collective-permute-start(bf16[3,1024]{1,0:T(4,128)(2,1)S(1)} %fusion.40), channel_id=1, source_target_pairs={{0,4},{4,8},{8,12},{12,16},{16,20},{20,24},{24,28},{28,32},{32,36}... | collective-permute-start | bytes 18440 | tf_op jit(solution)/shard_map/ppermute | solution.py:18
  140.1 2.3 copy-start.3
  140.9 1.9 copy-start.1
  143.2 1.4 copy-start.2
  144.6 7.4 %copy-start.4 = (f32[24,768]{1,0:T(8,128)S(1)}, f32[24,768]{1,0:T(8,128)}, u32[]{:S(2)}) copy-start(f32[24,768]{1,0:T(8,128)} %param.17) | copy-start | bytes 221188
  144.7 199.7 %all-to-all-start = ((bf16[768,64,24]{0,2,1:T(8,128)(2,1)}), bf16[768,64,24]{0,2,1:T(8,128)(2,1)S(1)}, u32[]{:S(2)}, u32[]{:S(2)}) async-start(bf16[768,64,24]{0,2,1:T(8,128)(2,1)} %bitcast.87), calls=%async_computation | async-start | bytes 4718592 | tf_op jit(solution)/shard_map/all_to_all | solution.py:12
  152.0 177.3 %all-gather.9.cloned.1.call-start = ((), (), s32[]{:S(2)}) async-start(), calls=%async_computation.3 | async-start | bytes 2396160 | tf_op jit(solution)/shard_map/all_gather | solution.py:103
  152.7 214.5 %reduce-scatter.4.cloned.1.call-start = ((), (), s32[]{:S(2)}) async-start(), calls=%async_computation.5 | async-start | bytes 983040
  255.2 70.0 %copy-start.9 = (f32[12]{0:T(128)S(1)}, f32[12]{0:T(128)}, u32[]{:S(2)}) copy-start(f32[12]{0:T(128)} %param.25) | copy-start | bytes 148
  329.2 15.1 %copy-start.6 = (f32[768]{0:T(1024)S(1)}, f32[768]{0:T(1024)}, u32[]{:S(2)}) copy-start(f32[768]{0:T(1024)} %param.26) | copy-start | bytes 9220
Sparse Core Ops, SparseCore 0:
  10.1 79.4 all-gather.6
  142.5 102.6 all-gather.10
  247.9 75.7 all-gather.8
  347.6 19.5 reduce-scatter.3
